TPU v7x, 32 devices: a whole 2x2x4 slice. The times are simulated.
32 devices in a mesh: pipe: 4 (over y, x), dp: 8 (over z, core).
Axes of the slice: x: 2, y: 2, z: 4, core: 2. Of those that a mesh axis runs over, the one named last changes fastest.
Arguments:
- cotangent: bfloat16 [4, 1024, 6144], P('pipe', 'dp'), may hold values from -0.29882812 to 0.29882812
- slot_token: int32 [4, 8, 24], P('pipe', 'dp'), may hold values from 0 to 127, as said below
- slot_count: int32 [4, 8], P('pipe', 'dp'), may hold values from 6 to 24, as said below
- slot_weight: float32 [4, 8, 24], P('pipe', 'dp'), may hold values from 0.1 to 0.9
- hidden: bfloat16 [4, 8, 24, 8192], P('pipe', 'dp'), may hold values from -6 to 6
Outputs:
- down_grad: bfloat16 [4, 8192, 6144], P('pipe', 'dp')
Inputs may be any that keep to these rules, and one draw needn't show every extreme that they name: `slot_token`: within one device's 24 slots of a section the token indices are distinct. `slot_count`: in every section some device has all 24 slots live.
All inputs are finite; a program needn't handle non-finite values.
Results may differ from a plain program's by a relative error of at most 0.0049.
Values may be sent and summed in bfloat16 or wider, within the bound.
No kernel may reach another device: no remote copies, remote signals or barrier semaphores. Data moves between devices by JAX's collectives and lax.ppermute only.
A program may use at most 128 MiB of HBM per device.

v0:
```python
import jax
import jax.numpy as jnp
from jax import lax
from jax.sharding import PartitionSpec as P


def shifted(value, axis, steps):
    count = lax.axis_size(axis)
    pairs = [(source, (source + steps) % count) for source in range(count)]
    return lax.ppermute(value, axis, pairs)


def select_rows(table, positions):
    return jnp.take(table[0], positions.reshape(-1), axis=0)


def local(cotangent, slot_token, slot_count, slot_weight, hidden):
    slots = slot_token.shape[2]
    slot_pos = lax.broadcasted_iota(jnp.int32, (slots,), 0)
    live_mask = (slot_pos < slot_count[0, 0]).astype(jnp.float32)
    ahead_tokens = shifted(slot_token, "pipe", 1)
    prepared = select_rows(cotangent, ahead_tokens)
    picked = shifted(prepared, "pipe", -1)
    factors = slot_weight[0, 0] * live_mask
    scaled_rows = (factors[:, None] * picked.astype(jnp.float32)).astype(jnp.bfloat16)[None]
    exchanged = lax.all_to_all(hidden, "dp", split_axis=3, concat_axis=1, tiled=True)[0]
    gathered = lax.all_gather(scaled_rows, "dp", axis=0, tiled=True)
    width = gathered.shape[2]
    flat_rows = gathered.reshape(-1, width)
    flat_hidden = exchanged.reshape(-1, exchanged.shape[2])
    summed = lax.dot_general(
        flat_hidden, flat_rows, (((0,), (0,)), ((), ())), preferred_element_type=jnp.float32
    )
    return summed.astype(jnp.bfloat16)[None]


def solution(mesh):
    placed = (
        P("pipe", "dp", None),
        P("pipe", "dp", None),
        P("pipe", "dp"),
        P("pipe", "dp", None),
        P("pipe", "dp", None, None),
    )
    return jax.shard_map(
        local, mesh=mesh, in_specs=placed, out_specs=P("pipe", "dp", None), check_vma=False
    )
```

profile of v0, /device:TPU:0, one launch (start us, length us, event | category | flops | bytes accessed | tf_op | source)
XLA Modules:
  0.0 143.8 jit_solution(2741923419532207530)
XLA Ops:
  6.5 0.0 copy-start
  6.5 0.0 all-gather.3.cloned.1.call-start
  6.5 3.0 %collective-permute-start = (s32[1,1,24]{2,1,0:T(1,128)}, s32[1,1,24]{2,1,0:T(1,128)S(1)}, u32[]{:S(2)}, u32[]{:S(2)}) collective-permute-start(s32[1,1,24]{2,1,0:T(1,128)} %param.6), channel_id=1, source_target_pairs={{0,8},{8,16},{16,24},{24,0},{1,9},{9,17},{17,25},{25,1},{2,10},{10... | collective-permute-start | bytes 296 | tf_op jit(solution)/shard_map/ppermute | solution.py:10
  9.6 2.6 %collective-permute-done = s32[1,1,24]{2,1,0:T(1,128)S(1)} collective-permute-done((s32[1,1,24]{2,1,0:T(1,128)}, s32[1,1,24]{2,1,0:T(1,128)S(1)}, u32[]{:S(2)}, u32[]{:S(2)}) %collective-permute-start) | collective-permute-done | bytes 128 | tf_op jit(solution)/shard_map/ppermute | solution.py:10
  12.2 0.0 copy-done
  12.2 0.7 gather_fusion
  13.0 0.1 broadcast_select_fusion
  13.1 2.1 %collective-permute-start.1 = (bf16[24,6144]{1,0:T(8,128)(2,1)S(1)}, bf16[24,6144]{1,0:T(8,128)(2,1)S(1)}, u32[]{:S(2)}, u32[]{:S(2)}) collective-permute-start(bf16[24,6144]{1,0:T(8,128)(2,1)S(1)} %broadcast_select_fusion), channel_id=1, source_target_pairs={{0,24},{8,0},{16,8},{24,16},{1,25},{9,1},{17,9},{25,17},{2,26},{10... | collective-permute-start | bytes 884744 | tf_op jit(solution)/shard_map/ppermute | solution.py:10
  15.8 0.0 copy-done.2
  15.8 5.2 %collective-permute-done.1 = bf16[24,6144]{1,0:T(8,128)(2,1)S(1)} collective-permute-done((bf16[24,6144]{1,0:T(8,128)(2,1)S(1)}, bf16[24,6144]{1,0:T(8,128)(2,1)S(1)}, u32[]{:S(2)}, u32[]{:S(2)}) %collective-permute-start.1) | collective-permute-done | bytes 294944 | tf_op jit(solution)/shard_map/ppermute | solution.py:10
  21.0 0.8 multiply_convert_fusion
  21.8 0.0 all-gather.3.cloned.1.call-update
  21.9 6.7 %copy.10 = bf16[1,1,24,8192]{2,1,0,3:T(2,128)(2,1)} copy(bf16[1,1,24,8192]{3,2,1,0:T(8,128)(2,1)S(1)} %copy-done.1) | data formatting | bytes 786432 | tf_op args[4]
  28.5 0.6 broadcast.49
  29.1 46.6 %reduce = bf16[8192,24]{1,0:T(8,128)(2,1)} reduce(bf16[8192,1,1,24]{3,2,1,0:T(2,128)(2,1)} %bitcast.28, bf16[]{:T(256)} %broadcast.49), dimensions={1,2}, to_apply=%bitcast.22.reduce_sub_computation | reduce | bytes 786434
  75.6 3.9 %reshape.65 = bf16[8,2,12288]{2,1,0:T(2,128)(2,1)S(1)} reshape(bf16[8192,24]{1,0:T(8,128)(2,1)} %reduce) | data formatting | bytes 786432
  79.6 17.4 %all_to_all.15 = bf16[8,2,12288]{2,1,0:T(2,128)(2,1)S(1)} all-to-all(bf16[8,2,12288]{2,1,0:T(2,128)(2,1)S(1)} %reshape.65), channel_id=1, replica_groups=mesh['pipe'=4,'dp'=8] {'dp'}, dimensions={0} | all-to-all | bytes 786432 | tf_op jit(solution)/shard_map/all_to_all | solution.py:26
  96.9 6.6 %reshape.66 = bf16[8192,1,1,24]{3,2,1,0:T(2,128)(2,1)} reshape(bf16[8,2,12288]{2,1,0:T(2,128)(2,1)S(1)} %all_to_all.15) | data formatting | bytes 786432
  103.6 8.0 %copy.11 = bf16[1,1,24,8192]{3,2,1,0:T(8,128)(2,1)S(1)} copy(bf16[1,1,24,8192]{2,1,0,3:T(2,128)(2,1)} %bitcast.29) | data formatting | bytes 786432 | tf_op jit(solution)/shard_map/all_to_all | solution.py:26
  111.6 0.2 copy.14
  111.8 0.2 copy.12
  112.1 0.0 all-gather.3.cloned.1.call-done
  112.1 8.3 %convert_bitcast_fusion = bf16[1,1024,6144]{1,2,0:T(8,128)(2,1)} fusion(bf16[192,6144]{1,0:T(8,128)(2,1)} %all-gather.3.cloned.1.call-done, bf16[192,1024]{1,0:T(8,128)(2,1)S(1)} %bitcast.32), kind=kOutput, calls=%fused_computation.1 | convolution fusion | flops 2422210560 | bytes 15335424 | tf_op jit(solution)/shard_map/dot_general | solution.py:31
  120.4 16.6 %copy.13 = bf16[1,1024,6144]{2,1,0:T(8,128)(2,1)} copy(bf16[1,1024,6144]{1,2,0:T(8,128)(2,1)} %convert_bitcast_fusion) | data formatting | bytes 25165824 | tf_op jit(solution)/shard_map/broadcast_in_dim | solution.py:34
  (7 shorter events, 0.0 us)
Async XLA Ops:
  6.5 5.7 %copy-start = (bf16[1,128,6144]{2,1,0:T(8,128)(2,1)S(1)}, bf16[1,128,6144]{2,1,0:T(8,128)(2,1)}, u32[]{:S(2)}) copy-start(bf16[1,128,6144]{2,1,0:T(8,128)(2,1)} %param.5) | copy-start | bytes 4718596
  6.5 9.3 %copy-start.2 = (f32[1,1,24]{2,1,0:T(1,128)S(1)}, f32[1,1,24]{2,1,0:T(1,128)}, u32[]{:S(2)}) copy-start(f32[1,1,24]{2,1,0:T(1,128)} %param.8) | copy-start | bytes 292
  6.5 15.3 %copy-start.1 = (bf16[1,1,24,8192]{3,2,1,0:T(8,128)(2,1)S(1)}, bf16[1,1,24,8192]{3,2,1,0:T(8,128)(2,1)}, u32[]{:S(2)}) copy-start(bf16[1,1,24,8192]{3,2,1,0:T(8,128)(2,1)} %param.9) | copy-start | bytes 1179652
  6.5 105.5 %all-gather.3.cloned.1.call-start = ((), (), s32[]{:S(2)}) async-start(), calls=%async_computation.1 | async-start | bytes 2654208 | tf_op jit(solution)/shard_map/all_gather | solution.py:27
  6.5 5.7 %collective-permute-start = (s32[1,1,24]{2,1,0:T(1,128)}, s32[1,1,24]{2,1,0:T(1,128)S(1)}, u32[]{:S(2)}, u32[]{:S(2)}) collective-permute-start(s32[1,1,24]{2,1,0:T(1,128)} %param.6), channel_id=1, source_target_pairs={{0,8},{8,16},{16,24},{24,0},{1,9},{9,17},{17,25},{25,1},{2,10},{10... | collective-permute-start | bytes 296 | tf_op jit(solution)/shard_map/ppermute | solution.py:10
  13.1 7.9 %collective-permute-start.1 = (bf16[24,6144]{1,0:T(8,128)(2,1)S(1)}, bf16[24,6144]{1,0:T(8,128)(2,1)S(1)}, u32[]{:S(2)}, u32[]{:S(2)}) collective-permute-start(bf16[24,6144]{1,0:T(8,128)(2,1)S(1)} %broadcast_select_fusion), channel_id=1, source_target_pairs={{0,24},{8,0},{16,8},{24,16},{1,25},{9,1},{17,9},{25,17},{2,26},{10... | collective-permute-start | bytes 884744 | tf_op jit(solution)/shard_map/ppermute | solution.py:10
Sparse Core Ops, SparseCore 0:
  22.0 32.8 all-gather.2
where the time goes:
time: 145 us; the launch traced here: 144 us
  other arithmetic  47.5 us (33%)
  local copies, waits for them, and re-layouts  43.5 us (30%)
  blocking collectives  17.4 us (12%)
  between operations  14.1 us (10%)
  matrix products  8.29 us (6%)
  waiting for transfers between devices  7.86 us (5%)
  starting transfers between devices  5.09 us (4%)
    unnamed x1, other arithmetic  46.6 us
    unnamed x11, local copies, waits for them, and re-layouts  18 us
    all_to_all x1, blocking collectives, local(): lax.all_to_all(hidden, 'dp', split_axis=3, concat_axis=1, tiled=True)[0]  17.4 us
    broadcast_in_dim x1, local copies, waits for them, and re-layouts, local(): return summed.astype(jnp.bfloat16)[None]  16.6 us
    dot_general x1, matrix products, local(): lax.dot_general(flat_hidden, flat_rows, (((0,), (0,)), ((), ())), preferr...  8.29 us
    all_to_all x2, local copies, waits for them, and re-layouts, local(): lax.all_to_all(hidden, 'dp', split_axis=3, concat_axis=1, tiled=True)[0]  8.22 us
    ppermute x2, waiting for transfers between devices, shifted(): return lax.ppermute(value, axis, pairs)  7.82 us
    ppermute x2, starting transfers between devices, shifted(): return lax.ppermute(value, axis, pairs)  5.09 us
  transfers between devices with their start and end apart: 3, of which 2 were waited for; matrix products, arithmetic and copies ran while one was open for 51% of the time, Pallas kernels for 0%

commit v1 on v0

--- a/solution.py
+++ b/solution.py
@@ -2,6 +2,12 @@
 import jax.numpy as jnp
 from jax import lax
 from jax.sharding import PartitionSpec as P
+
+
+def trade_parts(x, axis, split, join):
+    pieces = jnp.split(x, lax.axis_size(axis), axis=split)
+    got = lax.all_to_all(jnp.stack(pieces), axis, 0, 0)
+    return jnp.concatenate(got, axis=join)
 
 
 def shifted(value, axis, steps):
@@ -23,7 +29,7 @@
     picked = shifted(prepared, "pipe", -1)
     factors = slot_weight[0, 0] * live_mask
     scaled_rows = (factors[:, None] * picked.astype(jnp.float32)).astype(jnp.bfloat16)[None]
-    exchanged = lax.all_to_all(hidden, "dp", split_axis=3, concat_axis=1, tiled=True)[0]
+    exchanged = trade_parts(hidden, "dp", 3, 1)[0]
     gathered = lax.all_gather(scaled_rows, "dp", axis=0, tiled=True)
     width = gathered.shape[2]
     flat_rows = gathered.reshape(-1, width)

time: 145 us -> 75.1 us (0.52)
  other arithmetic: 47.5 us -> 0.95 us
  local copies, waits for them, and re-layouts: 43.5 us -> 0.78 us
  waiting for transfers between devices: 7.86 us -> 21.8 us
  blocking collectives: 17.4 us -> 23.9 us
    unnamed x1 -> x0, other arithmetic: 46.6 us -> none
    unnamed x11 -> x13, local copies, waits for them, and re-layouts: 18 us -> 0.05 us
    broadcast_in_dim x1 -> x0, local copies, waits for them, and re-layouts: 16.6 us -> none  [local(): return summed.astype(jnp.bfloat16)[None]]
    all_gather x1, waiting for transfers between devices: 0.02 us -> 14 us  [local(): gathered = lax.all_gather(scaled_rows, 'dp', axis=0, tiled=True)]
    all_to_all x2 -> x0, local copies, waits for them, and re-layouts: 8.22 us -> none  [local(): lax.all_to_all(hidden, 'dp', split_axis=3, concat_axis=1, tiled=True)[0]]
    all_to_all x1, blocking collectives: 17.4 us -> 23.9 us  [trade_parts(): got = lax.all_to_all(jnp.stack(pieces), axis, 0, 0)]
  transfers between devices with their start and end apart: 3 -> 3, of which waited for: 2 -> 3; matrix products, arithmetic and copies ran while one was open for 51% -> 0% of each run, Pallas kernels for 0% -> 0%
where the time goes in v1:
time: 75.1 us; the launch traced here: 75 us
  blocking collectives  23.9 us (32%)
  waiting for transfers between devices  21.8 us (29%)
  between operations  14.2 us (19%)
  matrix products  8.28 us (11%)
  starting transfers between devices  5.09 us (7%)
  other arithmetic  0.95 us (1%)
  local copies, waits for them, and re-layouts  0.78 us (1%)
    all_to_all x1, blocking collectives, trade_parts(): got = lax.all_to_all(jnp.stack(pieces), axis, 0, 0)  23.9 us
    all_gather x1, waiting for transfers between devices, local(): gathered = lax.all_gather(scaled_rows, 'dp', axis=0, tiled=True)  14 us
    dot_general x1, matrix products, local(): lax.dot_general(flat_hidden, flat_rows, (((0,), (0,)), ((), ())), preferr...  8.28 us
    ppermute x2, waiting for transfers between devices, shifted(): return lax.ppermute(value, axis, pairs)  7.82 us
    ppermute x2, starting transfers between devices, shifted(): return lax.ppermute(value, axis, pairs)  5.09 us
  transfers between devices with their start and end apart: 3, of which 3 were waited for; matrix products, arithmetic and copies ran while one was open for 0% of the time, Pallas kernels for 0%

profile of v1, /device:TPU:0, one launch (start us, length us, event | category | flops | bytes accessed | tf_op | source)
XLA Modules:
  0.0 75.0 jit_solution(2446186189634155103)
XLA Ops:
  6.5 0.0 copy-start
  6.5 0.0 copy-start.2
  6.5 0.0 copy-start.1
  6.5 0.0 all-gather.3.cloned.1.call-start
  6.5 3.0 %collective-permute-start = (s32[1,1,24]{2,1,0:T(1,128)}, s32[1,1,24]{2,1,0:T(1,128)S(1)}, u32[]{:S(2)}, u32[]{:S(2)}) collective-permute-start(s32[1,1,24]{2,1,0:T(1,128)} %param.6), channel_id=1, source_target_pairs={{0,8},{8,16},{16,24},{24,0},{1,9},{9,17},{17,25},{25,1},{2,10},{10... | collective-permute-start | bytes 296 | tf_op jit(solution)/shard_map/ppermute | solution.py:16
  9.6 2.6 %collective-permute-done = s32[1,1,24]{2,1,0:T(1,128)S(1)} collective-permute-done((s32[1,1,24]{2,1,0:T(1,128)}, s32[1,1,24]{2,1,0:T(1,128)S(1)}, u32[]{:S(2)}, u32[]{:S(2)}) %collective-permute-start) | collective-permute-done | bytes 128 | tf_op jit(solution)/shard_map/ppermute | solution.py:16
  12.2 0.0 copy-done
  12.2 0.7 gather_fusion
  13.0 0.1 broadcast_select_fusion
  13.1 2.1 %collective-permute-start.1 = (bf16[24,6144]{1,0:T(8,128)(2,1)S(1)}, bf16[24,6144]{1,0:T(8,128)(2,1)S(1)}, u32[]{:S(2)}, u32[]{:S(2)}) collective-permute-start(bf16[24,6144]{1,0:T(8,128)(2,1)S(1)} %broadcast_select_fusion), channel_id=1, source_target_pairs={{0,24},{8,0},{16,8},{24,16},{1,25},{9,1},{17,9},{25,17},{2,26},{10... | collective-permute-start | bytes 884744 | tf_op jit(solution)/shard_map/ppermute | solution.py:16
  15.8 0.0 copy-done.2
  15.8 5.2 %collective-permute-done.1 = bf16[24,6144]{1,0:T(8,128)(2,1)S(1)} collective-permute-done((bf16[24,6144]{1,0:T(8,128)(2,1)S(1)}, bf16[24,6144]{1,0:T(8,128)(2,1)S(1)}, u32[]{:S(2)}, u32[]{:S(2)}) %collective-permute-start.1) | collective-permute-done | bytes 294944 | tf_op jit(solution)/shard_map/ppermute | solution.py:16
  21.0 0.8 %multiply_convert_fusion = bf16[24,6144]{1,0:T(8,128)(2,1)} fusion(bf16[24,6144]{1,0:T(8,128)(2,1)S(1)} %collective-permute-done.1, f32[24]{0:T(128)S(1)} %compare_select_fusion.2), kind=kLoop, calls=%fused_computation.2 | loop fusion | flops 442368 | bytes 589920 | tf_op jit(solution)/shard_map/convert_element_type | solution.py:31
  21.8 0.0 all-gather.3.cloned.1.call-update
  21.9 0.0 copy-done.1
  22.0 23.9 %all_to_all.5 = bf16[8,1,1,24,1024]{4,3,2,1,0:T(8,128)(2,1)S(1)} all-to-all(bf16[8,1,1,24,1024]{4,3,2,1,0:T(8,128)(2,1)S(1)} %bitcast_dynamic-update-slice_fusion), channel_id=1, replica_groups=mesh['pipe'=4,'dp'=8] {'dp'}, dimensions={0} | all-to-all | bytes 786432 | tf_op jit(solution)/shard_map/all_to_all | solution.py:9
  45.8 14.0 %all-gather.3.cloned.1.call-done = bf16[192,6144]{1,0:T(8,128)(2,1)} async-done(((bf16[24,6144]{1,0:T(8,128)(2,1)}), bf16[192,6144]{1,0:T(8,128)(2,1)}) %all-gather.3.cloned.1.call-update) | async-done | bytes 2359312 | tf_op jit(solution)/shard_map/all_gather | solution.py:33
  59.8 8.3 %convert_bitcast_fusion = bf16[1,1024,6144]{2,1,0:T(8,128)(2,1)} fusion(bf16[192,1024]{1,0:T(8,128)(2,1)S(1)} %bitcast.33, bf16[192,6144]{1,0:T(8,128)(2,1)} %all-gather.3.cloned.1.call-done), kind=kOutput, calls=%fused_computation.1 | convolution fusion | flops 2422210560 | bytes 15335424 | tf_op jit(solution)/shard_map/dot_general | solution.py:37
  (12 shorter events, 0.1 us)
Async XLA Ops:
  6.5 5.7 %copy-start = (bf16[1,128,6144]{2,1,0:T(8,128)(2,1)S(1)}, bf16[1,128,6144]{2,1,0:T(8,128)(2,1)}, u32[]{:S(2)}) copy-start(bf16[1,128,6144]{2,1,0:T(8,128)(2,1)} %param.5) | copy-start | bytes 4718596
  6.5 9.3 %copy-start.2 = (f32[1,1,24]{2,1,0:T(1,128)S(1)}, f32[1,1,24]{2,1,0:T(1,128)}, u32[]{:S(2)}) copy-start(f32[1,1,24]{2,1,0:T(1,128)} %param.8) | copy-start | bytes 292
  6.5 15.3 %copy-start.1 = (bf16[1,1,24,8192]{3,2,1,0:T(8,128)(2,1)S(1)}, bf16[1,1,24,8192]{3,2,1,0:T(8,128)(2,1)}, u32[]{:S(2)}) copy-start(bf16[1,1,24,8192]{3,2,1,0:T(8,128)(2,1)} %param.9) | copy-start | bytes 1179652
  6.5 53.3 %all-gather.3.cloned.1.call-start = ((), (), s32[]{:S(2)}) async-start(), calls=%async_computation.1 | async-start | bytes 2654208 | tf_op jit(solution)/shard_map/all_gather | solution.py:33
  6.5 5.7 %collective-permute-start = (s32[1,1,24]{2,1,0:T(1,128)}, s32[1,1,24]{2,1,0:T(1,128)S(1)}, u32[]{:S(2)}, u32[]{:S(2)}) collective-permute-start(s32[1,1,24]{2,1,0:T(1,128)} %param.6), channel_id=1, source_target_pairs={{0,8},{8,16},{16,24},{24,0},{1,9},{9,17},{17,25},{25,1},{2,10},{10... | collective-permute-start | bytes 296 | tf_op jit(solution)/shard_map/ppermute | solution.py:16
  13.1 7.9 %collective-permute-start.1 = (bf16[24,6144]{1,0:T(8,128)(2,1)S(1)}, bf16[24,6144]{1,0:T(8,128)(2,1)S(1)}, u32[]{:S(2)}, u32[]{:S(2)}) collective-permute-start(bf16[24,6144]{1,0:T(8,128)(2,1)S(1)} %broadcast_select_fusion), channel_id=1, source_target_pairs={{0,24},{8,0},{16,8},{24,16},{1,25},{9,1},{17,9},{25,17},{2,26},{10... | collective-permute-start | bytes 884744 | tf_op jit(solution)/shard_map/ppermute | solution.py:16
Sparse Core Ops, SparseCore 0:
  22.0 37.8 all-gather.2
